TPU v7x, 32 devices: a whole 2x2x4 slice. The times are simulated.
32 devices in a mesh: dp: 16 (over z, x, core), mp: 2 (over y).
Axes of the slice: x: 2, y: 2, z: 4, core: 2. Of those that a mesh axis runs over, the one named last changes fastest.
Arguments:
- images: bfloat16 [64, 196, 512], P('dp'), may hold values from -6 to 6
- cotangent: bfloat16 [64, 196, 512], P('dp'), may hold values from -6 to 6
- w_query: bfloat16 [512, 512], P('dp', 'mp'), may hold values from -0.25 to 0.25
- w_key: bfloat16 [512, 512], P('dp', 'mp'), may hold values from -0.25 to 0.25
- w_value: bfloat16 [512, 512], P('dp', 'mp'), may hold values from -0.25 to 0.25
- w_proj: bfloat16 [512, 512], P('mp', 'dp'), may hold values from -1 to 1
- w_up: bfloat16 [512, 2048], P('dp', 'mp'), may hold values from -0.25 to 0.25
- w_down: bfloat16 [2048, 512], P('mp', 'dp'), may hold values from -0.125 to 0.125
- gains: bfloat16 [2, 512], P(None, 'dp'), may hold values from 0.25 to 1.75
- shifts: bfloat16 [4, 512], P(None, 'dp'), may hold values from -3 to 3
- qv_bias: bfloat16 [2, 512], P(None, 'mp'), may hold values from -3 to 3
- up_bias: bfloat16 [2048], P('mp'), may hold values from -3 to 3
- table: bfloat16 [16, 169], P('mp'), may hold values from -5 to 5
- regions: int32 [4, 49], replicated, may hold values from 0 to 3
- rel_index: int32 [49, 49], replicated, may hold values from 0 to 168
Outputs:
- output: bfloat16 [64, 196, 512], P('dp')
- d_images: bfloat16 [64, 196, 512], P('dp')
- g_query: float32 [512, 512], P('dp', 'mp')
- g_key: float32 [512, 512], P('dp', 'mp')
- g_value: float32 [512, 512], P('dp', 'mp')
- g_proj: float32 [512, 512], P('mp', 'dp')
- g_up: float32 [512, 2048], P('dp', 'mp')
- g_down: float32 [2048, 512], P('mp', 'dp')
- g_gains: float32 [2, 512], P(None, 'dp')
- g_shifts: float32 [4, 512], P(None, 'dp')
- g_qv_bias: float32 [2, 512], P(None, 'mp')
- g_up_bias: float32 [2048], P('mp')
- g_table: float32 [16, 169], P('mp')
Inputs may be any that keep to these rules, and one draw needn't show every extreme that they name: `regions`: a position's scores to positions of another region of its window get -100.
All inputs are finite; a program needn't handle non-finite values.
Results may differ from a plain program's by a relative error of at most 0.017.
Values may be sent and summed in bfloat16 or wider, within the bound.
No kernel may reach another device: no remote copies, remote signals or barrier semaphores. Data moves between devices by JAX's collectives and lax.ppermute only.
A program may use at most 128 MiB of HBM per device.

v0:
```python
import math
import jax
import jax.numpy as jnp
from jax import lax
from jax.sharding import PartitionSpec as P

HEAD_DIM = 32
SIDE = 14
WIN = 7
SHIFT = 3
MICRO = 2
WINDOWS = 4


def to_windows(source):
    image_count = source.shape[0]
    channels = source.shape[2]
    grid = source.reshape(image_count, SIDE, SIDE, channels)
    grid = jnp.roll(grid, (-SHIFT, -SHIFT), (1, 2))
    grid = grid.reshape(image_count, SIDE // WIN, WIN, SIDE // WIN, WIN, channels)
    return grid.transpose(0, 1, 3, 2, 4, 5).reshape(image_count * WINDOWS, WIN * WIN, channels)


def from_windows(source, image_count):
    channels = source.shape[2]
    grid = source.reshape(image_count, SIDE // WIN, SIDE // WIN, WIN, WIN, channels)
    grid = grid.transpose(0, 1, 3, 2, 4, 5).reshape(image_count, SIDE, SIDE, channels)
    grid = jnp.roll(grid, (SHIFT, SHIFT), (1, 2))
    return grid.reshape(image_count, SIDE * SIDE, channels)


def normalize(source, gain_row, shift_row):
    centred = source - jnp.mean(source, axis=-1, keepdims=True)
    inverse = lax.rsqrt(jnp.mean(centred * centred, axis=-1, keepdims=True) + 1e-05)
    unit_rows = centred * inverse
    return (unit_rows * gain_row + shift_row, unit_rows, inverse)


def norm_back(grad_in, unit_rows, inverse, gain_row):
    scaled = grad_in * gain_row
    return inverse * (
        scaled
        - jnp.mean(scaled, axis=-1, keepdims=True)
        - unit_rows * jnp.mean(scaled * unit_rows, axis=-1, keepdims=True)
    )


def gelu_slope(hidden):
    normal_cdf = 0.5 * (1.0 + lax.erf(hidden * (1.0 / math.sqrt(2.0))))
    density = jnp.exp(-0.5 * hidden * hidden) * (1.0 / math.sqrt(2.0 * math.pi))
    return normal_cdf + hidden * density


def inner(left_mat, right_mat):
    return lax.dot_general(
        left_mat, right_mat, (((0,), (0,)), ((), ())), preferred_element_type=jnp.float32
    )


def against(left_mat, right_mat):
    return lax.dot_general(
        left_mat, right_mat, (((1,), (1,)), ((), ())), preferred_element_type=jnp.float32
    )


def body(
    images,
    cotangent,
    w_query,
    w_key,
    w_value,
    w_proj,
    w_up,
    w_down,
    gains,
    shifts,
    qv_bias,
    up_bias,
    table,
    regions,
    rel_index,
):
    image_count = images.shape[0] // MICRO
    row_count = image_count * SIDE * SIDE
    model_width = images.shape[2]
    local_width = qv_bias.shape[1]
    local_heads = table.shape[0]
    up_width = up_bias.shape[0]
    window_tokens = regions.shape[1]
    window_count = image_count * WINDOWS
    score_scale = HEAD_DIM ** (-0.5)
    table_codes = jnp.arange(table.shape[1], dtype=jnp.int32)
    onehot = (rel_index.reshape(1, -1) == table_codes[:, None]).astype(jnp.float32)
    rel_bias = jnp.dot(table.astype(jnp.float32), onehot, precision=lax.Precision.HIGHEST).reshape(
        local_heads, window_tokens, window_tokens
    )
    region_mask = jnp.where(regions[:, :, None] == regions[:, None, :], 0.0, -100.0).astype(
        jnp.float32
    )
    query_bias = qv_bias[0].astype(jnp.float32)
    value_bias = qv_bias[1].astype(jnp.float32)
    up_float = up_bias.astype(jnp.float32)

    def logits_of(query_heads, key_heads):
        raw = (
            jnp.einsum(
                "wihd,wjhd->whij", query_heads, key_heads, preferred_element_type=jnp.float32
            )
            * score_scale
        )
        framed = raw.reshape(image_count, WINDOWS, local_heads, window_tokens, window_tokens)
        framed = framed + region_mask[None, :, None] + rel_bias[None, None]
        return framed.reshape(window_count, local_heads, window_tokens, window_tokens)

    acc_query = jnp.zeros((model_width, local_width), jnp.float32)
    acc_key = jnp.zeros((model_width, local_width), jnp.float32)
    acc_value = jnp.zeros((model_width, local_width), jnp.float32)
    acc_proj = jnp.zeros((local_width, model_width), jnp.float32)
    acc_up = jnp.zeros((model_width, up_width), jnp.float32)
    acc_down = jnp.zeros((up_width, model_width), jnp.float32)
    gain_acc = jnp.zeros((2, model_width), jnp.float32)
    shift_acc = jnp.zeros((4, model_width), jnp.float32)
    table_acc = jnp.zeros(table.shape, jnp.float32)
    qv_acc = jnp.zeros(qv_bias.shape, jnp.float32)
    up_bias_acc = jnp.zeros(up_bias.shape, jnp.float32)
    outputs_list = []
    input_grads = []
    for micro_step in range(MICRO):
        ahead = (
            lax.all_gather(w_query, "dp", axis=0, tiled=True),
            lax.all_gather(w_key, "dp", axis=0, tiled=True),
            lax.all_gather(w_value, "dp", axis=0, tiled=True),
            lax.all_gather(w_proj, "dp", axis=1, tiled=True),
            lax.all_gather(w_up, "dp", axis=0, tiled=True),
            lax.all_gather(w_down, "dp", axis=1, tiled=True),
            lax.all_gather(gains, "dp", axis=1, tiled=True),
            lax.all_gather(shifts, "dp", axis=1, tiled=True),
        )
        full_query, full_key, full_value, full_proj, full_up, full_down, full_gains, full_shifts = (
            ahead
        )
        gain_rows = full_gains.astype(jnp.float32)
        shift_rows = full_shifts.astype(jnp.float32)
        first_row = micro_step * image_count
        source = images[first_row : first_row + image_count].astype(jnp.float32)
        normed_one, unit_one, inverse_one = normalize(source, gain_rows[0], shift_rows[0])
        window_rows = to_windows(normed_one.astype(jnp.bfloat16)).reshape(row_count, model_width)
        queries = (
            jnp.dot(window_rows, full_query, preferred_element_type=jnp.float32) + query_bias
        ).astype(jnp.bfloat16)
        key_rows = jnp.dot(window_rows, full_key, preferred_element_type=jnp.float32).astype(
            jnp.bfloat16
        )
        values = (
            jnp.dot(window_rows, full_value, preferred_element_type=jnp.float32) + value_bias
        ).astype(jnp.bfloat16)
        query_heads = queries.reshape(window_count, window_tokens, local_heads, HEAD_DIM)
        key_heads = key_rows.reshape(window_count, window_tokens, local_heads, HEAD_DIM)
        value_heads = values.reshape(window_count, window_tokens, local_heads, HEAD_DIM)
        logits = logits_of(query_heads, key_heads)
        row_max = jnp.max(logits, axis=-1, keepdims=True)
        log_total = row_max + jnp.log(jnp.sum(jnp.exp(logits - row_max), axis=-1, keepdims=True))
        soft_low = jnp.exp(logits - log_total).astype(jnp.bfloat16)
        mixed_out = jnp.einsum(
            "whij,wjhd->wihd", soft_low, value_heads, preferred_element_type=jnp.float32
        ).astype(jnp.bfloat16)
        token_mixed = from_windows(
            mixed_out.reshape(window_count, window_tokens, local_width), image_count
        ).reshape(row_count, local_width)
        projected = jnp.dot(token_mixed, full_proj, preferred_element_type=jnp.float32)
        source_rows = source.reshape(row_count, model_width)
        branch = lax.psum(projected, "mp") + shift_rows[2]
        middle = source_rows + branch
        normed_two, unit_two, inverse_two = normalize(middle, gain_rows[1], shift_rows[1])
        normed_low = normed_two.astype(jnp.bfloat16)
        hidden = jnp.dot(normed_low, full_up, preferred_element_type=jnp.float32) + up_float
        active = jax.nn.gelu(hidden, approximate=False).astype(jnp.bfloat16)
        lowered = jnp.dot(active, full_down, preferred_element_type=jnp.float32)
        outward = lax.psum(lowered.astype(jnp.bfloat16), "mp").astype(jnp.float32) + shift_rows[3]
        finished = (middle + outward).astype(jnp.bfloat16)
        outputs_list.append(finished.reshape(source.shape))
        behind = (
            lax.all_gather(w_query, "dp", axis=0, tiled=True),
            lax.all_gather(w_key, "dp", axis=0, tiled=True),
            lax.all_gather(w_value, "dp", axis=0, tiled=True),
            lax.all_gather(w_proj, "dp", axis=1, tiled=True),
            lax.all_gather(w_up, "dp", axis=0, tiled=True),
            lax.all_gather(w_down, "dp", axis=1, tiled=True),
            lax.all_gather(gains, "dp", axis=1, tiled=True),
            lax.all_gather(shifts, "dp", axis=1, tiled=True),
        )
        back_query, back_key, back_value, back_proj, back_up, back_down, back_gains, back_shifts = (
            behind
        )
        back_gain_rows = back_gains.astype(jnp.float32)
        grad_low = cotangent[first_row : first_row + image_count].reshape(row_count, model_width)
        grad_out = grad_low.astype(jnp.float32)
        acc_down = acc_down + inner(active, grad_low)
        grad_hidden = (against(grad_low, back_down) * gelu_slope(hidden)).astype(jnp.bfloat16)
        up_bias_acc = up_bias_acc + jnp.sum(grad_hidden.astype(jnp.float32), axis=0)
        acc_up = acc_up + inner(normed_low, grad_hidden)
        lifted = against(grad_hidden, back_up)
        grad_normed_two = lax.psum(lifted, "mp")
        shift_acc = shift_acc.at[3].add(jnp.sum(grad_out, axis=0))
        gain_acc = gain_acc.at[1].add(jnp.sum(grad_normed_two * unit_two, axis=0))
        shift_acc = shift_acc.at[1].add(jnp.sum(grad_normed_two, axis=0))
        grad_middle = grad_out + norm_back(
            grad_normed_two, unit_two, inverse_two, back_gain_rows[1]
        )
        shift_acc = shift_acc.at[2].add(jnp.sum(grad_middle, axis=0))
        grad_branch = grad_middle.astype(jnp.bfloat16)
        acc_proj = acc_proj + inner(token_mixed, grad_branch)
        grad_token = against(grad_branch, back_proj).astype(jnp.bfloat16)
        grad_mixed = to_windows(grad_token.reshape(image_count, SIDE * SIDE, local_width)).reshape(
            window_count, window_tokens, local_heads, HEAD_DIM
        )
        soft_again = jnp.exp(logits_of(query_heads, key_heads) - log_total)
        soft_again_low = soft_again.astype(jnp.bfloat16)
        grad_values = (
            jnp.einsum(
                "whij,wihd->wjhd", soft_again_low, grad_mixed, preferred_element_type=jnp.float32
            )
            .astype(jnp.bfloat16)
            .reshape(row_count, local_width)
        )
        grad_soft = jnp.einsum(
            "wihd,wjhd->whij", grad_mixed, value_heads, preferred_element_type=jnp.float32
        )
        grad_logits = soft_again * (
            grad_soft - jnp.sum(grad_soft * soft_again, axis=-1, keepdims=True)
        )
        table_acc = table_acc + jnp.dot(
            jnp.sum(grad_logits, axis=0).reshape(local_heads, -1),
            onehot.T,
            precision=lax.Precision.HIGHEST,
        )
        grad_scores = grad_logits.astype(jnp.bfloat16)
        grad_queries = (
            (
                jnp.einsum(
                    "whij,wjhd->wihd", grad_scores, key_heads, preferred_element_type=jnp.float32
                )
                * score_scale
            )
            .astype(jnp.bfloat16)
            .reshape(row_count, local_width)
        )
        grad_keys = (
            (
                jnp.einsum(
                    "whij,wihd->wjhd", grad_scores, query_heads, preferred_element_type=jnp.float32
                )
                * score_scale
            )
            .astype(jnp.bfloat16)
            .reshape(row_count, local_width)
        )
        qv_acc = qv_acc + jnp.stack(
            [
                jnp.sum(grad_queries.astype(jnp.float32), axis=0),
                jnp.sum(grad_values.astype(jnp.float32), axis=0),
            ]
        )
        acc_query = acc_query + inner(window_rows, grad_queries)
        acc_key = acc_key + inner(window_rows, grad_keys)
        acc_value = acc_value + inner(window_rows, grad_values)
        grad_window = (
            against(grad_queries, back_query)
            + against(grad_keys, back_key)
            + against(grad_values, back_value)
        )
        token_terms = from_windows(
            grad_window.reshape(window_count, window_tokens, model_width), image_count
        ).reshape(row_count, model_width)
        unit_one_rows = unit_one.reshape(row_count, model_width)
        inverse_rows = inverse_one.reshape(row_count, 1)
        grad_normed_one = lax.psum(token_terms, "mp")
        gain_acc = gain_acc.at[0].add(jnp.sum(grad_normed_one * unit_one_rows, axis=0))
        shift_acc = shift_acc.at[0].add(jnp.sum(grad_normed_one, axis=0))
        grad_source = grad_middle + norm_back(
            grad_normed_one, unit_one_rows, inverse_rows, back_gain_rows[0]
        )
        finished_grad = grad_source.astype(jnp.bfloat16)
        input_grads.append(finished_grad.reshape(source.shape))
    owned = (
        lax.psum_scatter(
            acc_query.astype(jnp.bfloat16), "dp", scatter_dimension=0, tiled=True
        ).astype(jnp.float32),
        lax.psum_scatter(
            acc_key.astype(jnp.bfloat16), "dp", scatter_dimension=0, tiled=True
        ).astype(jnp.float32),
        lax.psum_scatter(
            acc_value.astype(jnp.bfloat16), "dp", scatter_dimension=0, tiled=True
        ).astype(jnp.float32),
        lax.psum_scatter(
            acc_proj.astype(jnp.bfloat16), "dp", scatter_dimension=1, tiled=True
        ).astype(jnp.float32),
        lax.psum_scatter(acc_up.astype(jnp.bfloat16), "dp", scatter_dimension=0, tiled=True).astype(
            jnp.float32
        ),
        lax.psum_scatter(
            acc_down.astype(jnp.bfloat16), "dp", scatter_dimension=1, tiled=True
        ).astype(jnp.float32),
        lax.psum_scatter(
            gain_acc.astype(jnp.bfloat16), "dp", scatter_dimension=1, tiled=True
        ).astype(jnp.float32),
        lax.psum_scatter(
            shift_acc.astype(jnp.bfloat16), "dp", scatter_dimension=1, tiled=True
        ).astype(jnp.float32),
    )
    head_sums = lax.psum((table_acc, qv_acc, up_bias_acc), "dp")
    return (
        jnp.concatenate(outputs_list, axis=0),
        jnp.concatenate(input_grads, axis=0),
        owned[0],
        owned[1],
        owned[2],
        owned[3],
        owned[4],
        owned[5],
        owned[6],
        owned[7],
        head_sums[1],
        head_sums[2],
        head_sums[0],
    )


def solution(mesh):
    return jax.shard_map(
        body,
        mesh=mesh,
        in_specs=(
            P("dp", None, None),
            P("dp", None, None),
            P("dp", "mp"),
            P("dp", "mp"),
            P("dp", "mp"),
            P("mp", "dp"),
            P("dp", "mp"),
            P("mp", "dp"),
            P(None, "dp"),
            P(None, "dp"),
            P(None, "mp"),
            P("mp"),
            P("mp", None),
            P(),
            P(),
        ),
        out_specs=(
            P("dp", None, None),
            P("dp", None, None),
            P("dp", "mp"),
            P("dp", "mp"),
            P("dp", "mp"),
            P("mp", "dp"),
            P("dp", "mp"),
            P("mp", "dp"),
            P(None, "dp"),
            P(None, "dp"),
            P(None, "mp"),
            P("mp"),
            P("mp", None),
        ),
        check_vma=False,
    )
```

profile of v0, /device:TPU:0, one launch (start us, length us, event | category | flops | bytes accessed | tf_op | source)
XLA Modules:
  0.0 806.4 jit_solution(6925962472406569646)
XLA Ops:
  8.1 23.4 %all-gather = bf16[16,32,2]{1,2,0:T(2,128)(2,1)S(1)} all-gather(bf16[1,32,2]{1,2,0:T(2,128)(2,1)} %bitcast.263), channel_id=1, replica_groups=mesh['dp'=16,'mp'=2] {'dp'}, dimensions={0}, use_global_device_ids=true | all-gather | bytes 2176 | tf_op jit(solution)/shard_map/all_gather | solution.py:136
  31.6 17.7 %all-gather.1 = bf16[16,32,4]{1,2,0:T(4,128)(2,1)S(1)} all-gather(bf16[1,32,4]{1,2,0:T(4,128)(2,1)} %bitcast.262), channel_id=1, replica_groups=mesh['dp'=16,'mp'=2] {'dp'}, dimensions={0}, use_global_device_ids=true | all-gather | bytes 4352 | tf_op jit(solution)/shard_map/all_gather | solution.py:137
  54.4 2.8 subtract_multiply_fusion.4
  57.9 19.4 %all_gather.19 = bf16[512,256]{1,0:T(8,128)(2,1)S(1)} all-gather(bf16[32,256]{1,0:T(8,128)(2,1)S(1)} %copy-done.61), channel_id=1, replica_groups=mesh['dp'=16,'mp'=2] {'dp'}, dimensions={0}, use_global_device_ids=true | all-gather | bytes 278528 | tf_op jit(solution)/shard_map/all_gather | solution.py:130
  77.4 18.2 %all_gather.18 = bf16[512,256]{1,0:T(8,128)(2,1)S(1)} all-gather(bf16[32,256]{1,0:T(8,128)(2,1)S(1)} %copy-done.62), channel_id=1, replica_groups=mesh['dp'=16,'mp'=2] {'dp'}, dimensions={0}, use_global_device_ids=true | all-gather | bytes 278528 | tf_op jit(solution)/shard_map/all_gather | solution.py:132
  100.4 19.6 %all_gather.20 = bf16[512,256]{1,0:T(8,128)(2,1)S(1)} all-gather(bf16[32,256]{1,0:T(8,128)(2,1)S(1)} %copy-done.63), channel_id=1, replica_groups=mesh['dp'=16,'mp'=2] {'dp'}, dimensions={0}, use_global_device_ids=true | all-gather | bytes 278528 | tf_op jit(solution)/shard_map/all_gather | solution.py:131
  132.7 3.2 copy.278
  159.6 3.2 copy.294
  162.9 2.8 reshape_reshape.46
  168.2 19.6 %all_gather.21 = bf16[256,512]{0,1:T(8,128)(2,1)} all-gather(bf16[256,32]{0,1:T(8,128)(2,1)S(1)} %copy-done.64), channel_id=1, replica_groups=mesh['dp'=16,'mp'=2] {'dp'}, dimensions={1}, use_global_device_ids=true | all-gather | bytes 278528 | tf_op jit(solution)/shard_map/all_gather | solution.py:133
  209.4 40.9 %all-reduce.15.cloned.1.call-done = (f32[392,512]{1,0:T(8,128)}, f32[392,512]{1,0:T(8,128)}) async-done(((f32[392,512]{1,0:T(8,128)}, f32[392,512]{1,0:T(8,128)}), (f32[392,512]{1,0:T(8,128)}, f32[392,512]{1,0:T(8,128)})) %all-reduce.15.cloned.1.call-update) | async-done | bytes 1605648 | tf_op jit(solution)/shard_map/psum | solution.py:172
  253.7 3.1 fusion.85
  256.7 20.5 %all-gather.7.cloned.1.call-done = bf16[1024,512]{0,1:T(8,128)(2,1)} async-done(((bf16[1024,32]{0,1:T(8,128)(2,1)}), bf16[1024,512]{0,1:T(8,128)(2,1)}) %all-gather.7.cloned.1.call-update) | async-done | bytes 1048592 | tf_op jit(solution)/shard_map/all_gather | solution.py:135
  277.2 3.5 convert_reduce_fusion
  283.2 9.1 %fusion.4 = (bf16[392,1024]{1,0:T(8,128)(2,1)}, bf16[392,1024]{1,0:T(8,128)(2,1)}, f32[392,1024]{1,0:T(8,128)S(1)}) fusion(f32[1024]{0:T(1024)S(1)} %convert_element_type.258, f32[392,1024]{1,0:T(8,128)S(1)} %copy-done.43, bf16[512,1024]{1,0:T(8,128)(2,1)S(1)} %copy-done.44, f32[392,512]{1,0:T(8,128)S(1)} %copy-done.8, f32[512]{0:T(512)S(1)} %bitcast.236, ...), kind=kOutput, calls=%fused_computation.22 | convolution fusion | flops 465031168 | bytes 6679616 | tf_op jit(solution)/shard_map/dot_general | solution.py:176
  296.5 3.0 convolution_convert_fusion.5
  309.3 38.5 %all-reduce.13.cloned.1.call-done = (f32[392,512]{1,0:T(8,128)}, f32[392,512]{1,0:T(8,128)}) async-done(((f32[392,512]{1,0:T(8,128)}, f32[392,512]{1,0:T(8,128)}), (f32[392,512]{1,0:T(8,128)}, f32[392,512]{1,0:T(8,128)})) %all-reduce.13.cloned.1.call-update) | async-done | bytes 1605648 | tf_op jit(solution)/shard_map/psum | solution.py:203
  347.8 3.1 multiply_reduce_fusion.4
  350.9 34.0 %all-reduce.17.cloned.1.call-done = (bf16[392,512]{1,0:T(8,128)(2,1)}, bf16[392,512]{1,0:T(8,128)(2,1)}) async-done(((bf16[392,512]{1,0:T(8,128)(2,1)}, bf16[392,512]{1,0:T(8,128)(2,1)}), (bf16[392,512]{1,0:T(8,128)(2,1)}, bf16[392,512]{1,0:T(8,128)(2,1)})) %all-reduce.17.cloned.1.call-update) | async-done | bytes 802832 | tf_op jit(solution)/shard_map/psum | solution.py:179
  385.0 4.3 fusion.88
  404.7 2.8 copy.300
  407.5 3.1 convert_reduce_fusion.4
  410.7 2.7 multiply_reduce_fusion.1
  416.9 2.8 copy.317
  419.7 3.1 convert_reduce_fusion.2
  480.7 3.0 convert_reduce_fusion.6
  504.2 61.3 %all-reduce.1 = (f32[2,256]{1,0:T(2,128)}, f32[1024]{0:T(1024)}, f32[8,169]{1,0:T(8,128)}) all-reduce(f32[2,256]{1,0:T(2,128)S(1)} %maximum_add_fusion, f32[1024]{0:T(1024)S(1)} %add.504, f32[8,169]{1,0:T(8,128)S(1)} %fusion.56), channel_id=1, replica_groups=mesh['dp'=16,'mp'=2] {'dp'}, use_global_device_ids=true, to_apply=%region_54.55 | all-reduce | flops 2888 | bytes 23104 | tf_op jit(solution)/shard_map/psum | solution.py:311
  568.1 51.5 %reduce-scatter.13.cloned.1.call-done = bf16[32,256]{1,0:T(8,128)(2,1)} async-done(((bf16[512,256]{1,0:T(8,128)(2,1)}), bf16[32,256]{1,0:T(8,128)(2,1)}) %reduce-scatter.13.cloned.1.call-update) | async-done | bytes 16400 | tf_op jit(solution)/shard_map/reduce_scatter | solution.py:286
  620.9 56.9 %reduce-scatter.15.cloned.1.call-done = bf16[32,256]{1,0:T(8,128)(2,1)} async-done(((bf16[512,256]{1,0:T(8,128)(2,1)}), bf16[32,256]{1,0:T(8,128)(2,1)}) %reduce-scatter.15.cloned.1.call-update) | async-done | bytes 16400 | tf_op jit(solution)/shard_map/reduce_scatter | solution.py:289
  680.8 2.6 multiply_reduce_fusion.2
  688.6 50.8 %reduce-scatter.25.cloned.1.call-done = bf16[32,2]{1,0:T(8,128)(2,1)} async-done(((bf16[512,2]{1,0:T(8,128)(2,1)}), bf16[32,2]{1,0:T(8,128)(2,1)}) %reduce-scatter.25.cloned.1.call-update) | async-done | bytes 144
  740.7 56.8 %reduce-scatter.27.cloned.1.call-done = bf16[32,4]{1,0:T(8,128)(2,1)} async-done(((bf16[512,4]{1,0:T(8,128)(2,1)}), bf16[32,4]{1,0:T(8,128)(2,1)}) %reduce-scatter.27.cloned.1.call-update) | async-done | bytes 272
  (429 shorter events, 201.9 us)
Async XLA Ops:
  8.0 113.9 %copy-start = (bf16[8,169]{1,0:T(8,128)(2,1)S(1)}, bf16[8,169]{1,0:T(8,128)(2,1)}, u32[]{:S(2)}) copy-start(bf16[8,169]{1,0:T(8,128)(2,1)} %param.51) | copy-start | bytes 8116
  8.0 44.3 %copy-start.4 = (bf16[4,196,512]{2,0,1:T(4,128)(2,1)S(1)}, bf16[4,196,512]{2,0,1:T(4,128)(2,1)}, u32[]{:S(2)}) copy-start(bf16[4,196,512]{2,0,1:T(4,128)(2,1)} %param.39) | copy-start | bytes 2408452
  8.0 242.3 %all-reduce.15.cloned.1.call-start = ((), (), s32[]{:S(2)}) async-start(), calls=%async_computation.20 | async-start | bytes 3211264 | tf_op jit(solution)/shard_map/psum | solution.py:172
  57.2 20.1 %copy-start.62 = (bf16[32,256]{1,0:T(8,128)(2,1)S(1)}, bf16[32,256]{1,0:T(8,128)(2,1)}, u32[]{:S(2)}) copy-start(bf16[32,256]{1,0:T(8,128)(2,1)} %param.43) | copy-start | bytes 49156
  77.4 20.8 %copy-start.12 = (bf16[512,256]{1,0:T(8,128)(2,1)}, bf16[512,256]{1,0:T(8,128)(2,1)S(1)}, u32[]{:S(2)}) copy-start(bf16[512,256]{1,0:T(8,128)(2,1)S(1)} %all_gather.19) | copy-start | bytes 786436
  99.4 22.3 %copy-start.56 = (s32[49,49]{1,0:T(8,128)S(1)}, s32[49,49]{1,0:T(8,128)}, u32[]{:S(2)}) copy-start(s32[49,49]{1,0:T(8,128)} %param.53) | copy-start | bytes 28816
  99.4 22.4 %copy-start.71 = (s32[4,49]{1,0:T(4,128)S(1)}, s32[4,49]{1,0:T(4,128)}, u32[]{:S(2)}) copy-start(s32[4,49]{1,0:T(4,128)} %param.52) | copy-start | bytes 2356
  159.6 8.6 %copy-start.64 = (bf16[256,32]{0,1:T(8,128)(2,1)S(1)}, bf16[256,32]{0,1:T(8,128)(2,1)}, u32[]{:S(2)}) copy-start(bf16[256,32]{0,1:T(8,128)(2,1)} %param.44) | copy-start | bytes 49156
  199.6 54.1 %all-gather.5.cloned.1.call-start = ((), (), s32[]{:S(2)}) async-start(), calls=%async_computation.8 | async-start | bytes 1114112 | tf_op jit(solution)/shard_map/all_gather | solution.py:134
  200.2 77.1 %all-gather.7.cloned.1.call-start = ((), (), s32[]{:S(2)}) async-start(), calls=%async_computation.9 | async-start | bytes 1114112 | tf_op jit(solution)/shard_map/all_gather | solution.py:135
  200.8 147.1 %all-reduce.13.cloned.1.call-start = ((), (), s32[]{:S(2)}) async-start(), calls=%async_computation.19 | async-start | bytes 3211264 | tf_op jit(solution)/shard_map/psum | solution.py:203
  283.2 9.2 %copy-start.28 = (bf16[392,512]{1,0:T(8,128)(2,1)S(1)}, bf16[392,512]{1,0:T(8,128)(2,1)}, u32[]{:S(2)}) copy-start(bf16[392,512]{1,0:T(8,128)(2,1)} %reshape.591) | copy-start | bytes 1204228
  283.2 9.2 %copy-start.78 = (bf16[1024,512]{0,1:T(8,128)(2,1)S(1)}, bf16[1024,512]{0,1:T(8,128)(2,1)}, u32[]{:S(2)}) copy-start(bf16[1024,512]{0,1:T(8,128)(2,1)} %all-gather.7.cloned.1.call-done) | copy-start | bytes 3145732
  296.4 88.6 %all-reduce.17.cloned.1.call-start = ((), (), s32[]{:S(2)}) async-start(), calls=%async_computation.21 | async-start | bytes 1605632 | tf_op jit(solution)/shard_map/psum | solution.py:179
  300.8 182.8 %reduce-scatter.21.cloned.1.call-start = ((), (), s32[]{:S(2)}) async-start(), calls=%async_computation.14 | async-start | bytes 1114112 | tf_op jit(solution)/shard_map/reduce_scatter | solution.py:298
  305.3 179.9 %reduce-scatter.23.cloned.1.call-start = ((), (), s32[]{:S(2)}) async-start(), calls=%async_computation.15 | async-start | bytes 1114112 | tf_op jit(solution)/shard_map/reduce_scatter | solution.py:301
  309.3 256.2 %reduce-scatter.19.cloned.1.call-start = ((), (), s32[]{:S(2)}) async-start(), calls=%async_computation.13 | async-start | bytes 278528 | tf_op jit(solution)/shard_map/reduce_scatter | solution.py:295
  347.8 37.1 %copy-start.70 = (f32[1,512]{1,0:T(1,128)S(1)}, f32[1,512]{1,0:T(1,128)}, u32[]{:S(2)}) copy-start(f32[1,512]{1,0:T(1,128)} %get-tuple-element.266) | copy-start | bytes 6148
  385.0 5.2 copy-start.11
  389.2 6.6 copy-start.9
  434.6 6.6 copy-start.33
  447.1 119.6 %reduce-scatter.17.cloned.1.call-start = ((), (), s32[]{:S(2)}) async-start(), calls=%async_computation.12 | async-start | bytes 278528 | tf_op jit(solution)/shard_map/reduce_scatter | solution.py:292
  451.5 4.6 copy-start.15
  451.5 168.1 %reduce-scatter.13.cloned.1.call-start = ((), (), s32[]{:S(2)}) async-start(), calls=%async_computation.10 | async-start | bytes 278528 | tf_op jit(solution)/shard_map/reduce_scatter | solution.py:286
  458.6 219.2 %reduce-scatter.15.cloned.1.call-start = ((), (), s32[]{:S(2)}) async-start(), calls=%async_computation.11 | async-start | bytes 278528 | tf_op jit(solution)/shard_map/reduce_scatter | solution.py:289
  461.1 218.0 %all-reduce.11.cloned.1.call-start = ((), (), s32[]{:S(2)}) async-start(), calls=%async_computation.18 | async-start | bytes 3211264 | tf_op jit(solution)/shard_map/psum | solution.py:277
  475.1 264.2 %reduce-scatter.25.cloned.1.call-start = ((), (), s32[]{:S(2)}) async-start(), calls=%async_computation.16 | async-start | bytes 139264
  491.6 4.5 copy-start.60
  491.6 8.4 %copy-start.67 = (f32[512]{0:T(512)S(1)}, f32[512]{0:T(512)}, u32[]{:S(2)}) copy-start(f32[512]{0:T(512)} %get-tuple-element.271) | copy-start | bytes 6148
  497.8 183.0 %copy-start.69 = (f32[392]{0:T(512)S(1)}, f32[392]{0:T(512)}, u32[]{:S(2)}) copy-start(f32[392]{0:T(512)} %rsqrt.50) | copy-start | bytes 4708
  684.6 112.9 %reduce-scatter.27.cloned.1.call-start = ((), (), s32[]{:S(2)}) async-start(), calls=%async_computation.17 | async-start | bytes 139264
  687.2 111.7 %copy-start.1 = (bf16[8,169]{1,0:T(8,128)(2,1)S(1)}, bf16[8,169]{1,0:T(8,128)(2,1)}, u32[]{:S(2)}) copy-start(bf16[8,169]{1,0:T(8,128)(2,1)} %param.51) | copy-start | bytes 8116
  (63 other events, 152.9 us)
Sparse Core Ops, SparseCore 0:
  199.7 50.5 all-reduce.14
  296.5 51.2 all-reduce.12
  350.2 34.7 all-reduce.16
  475.2 52.2 all-reduce.10
Sparse Core Ops, SparseCore 1:
  202.2 36.1 all-gather.4
  240.4 36.8 all-gather.6
  305.4 56.5 reduce-scatter.20
  365.6 56.6 reduce-scatter.22
  447.2 55.7 reduce-scatter.18
  506.5 54.8 reduce-scatter.16
  564.7 54.8 reduce-scatter.12
  623.0 54.8 reduce-scatter.14
  684.6 54.6 reduce-scatter.24
  742.8 54.6 reduce-scatter.26
where the time goes:
time: 815 us; the launch traced here: 806 us
  waiting for transfers between devices  351 us (43%)
  blocking collectives  179 us (22%)
  local copies, waits for them, and re-layouts  118 us (14%)
  matrix products  90.9 us (11%)
  other arithmetic  49.2 us (6%)
  between operations  17.1 us (2%)
    unnamed x16, waiting for transfers between devices  109 us
    psum x1, blocking collectives, body(): head_sums = lax.psum((table_acc, qv_acc, up_bias_acc), 'dp')  61.3 us
    reduce_scatter x1, waiting for transfers between devices, body(): lax.psum_scatter(acc_key.astype(jnp.bfloat16), 'dp', scatter_dimension=0,...  56.9 us
    reduce_scatter x1, waiting for transfers between devices, body(): lax.psum_scatter(acc_query.astype(jnp.bfloat16), 'dp', scatter_dimension=...  51.5 us
    psum x1, waiting for transfers between devices, body(): branch = lax.psum(projected, 'mp') + shift_rows[2]  40.9 us
    psum x1, waiting for transfers between devices, body(): grad_normed_two = lax.psum(lifted, 'mp')  38.5 us
    psum x1, waiting for transfers between devices, body(): lax.psum(lowered.astype(jnp.bfloat16), 'mp').astype(jnp.float32)  34 us
    all_gather x1, blocking collectives, body(): lax.all_gather(gains, 'dp', axis=1, tiled=True)  23.4 us
  transfers between devices with their start and end apart: 14, of which 8 were waited for; matrix products, arithmetic and copies ran while one was open for 19% of the time, Pallas kernels for 0%

commit v1 on v0

--- a/solution.py
+++ b/solution.py
@@ -3,6 +3,7 @@
 import jax.numpy as jnp
 from jax import lax
 from jax.sharding import PartitionSpec as P
+from jax.lax import all_gather
 
 HEAD_DIM = 32
 SIDE = 14
@@ -169,7 +170,7 @@
         ).reshape(row_count, local_width)
         projected = jnp.dot(token_mixed, full_proj, preferred_element_type=jnp.float32)
         source_rows = source.reshape(row_count, model_width)
-        branch = lax.psum(projected, "mp") + shift_rows[2]
+        branch = all_gather(projected, "mp").sum(axis=0) + shift_rows[2]
         middle = source_rows + branch
         normed_two, unit_two, inverse_two = normalize(middle, gain_rows[1], shift_rows[1])
         normed_low = normed_two.astype(jnp.bfloat16)

time: 815 us -> 952 us (1.17)
  waiting for transfers between devices: 351 us -> 484 us
    psum x1, waiting for transfers between devices: 0.01 us -> 53 us  [body(): grad_normed_one = lax.psum(token_terms, 'mp')]
    psum x1 -> x0, waiting for transfers between devices: 40.9 us -> none  [body(): branch = lax.psum(projected, 'mp') + shift_rows[2]]
    reduce_scatter x1, waiting for transfers between devices: 0.01 us -> 38.8 us  [body(): lax.psum_scatter(acc_value.astype(jnp.bfloat16), 'dp', scatter_dimension=...]
    reduce_scatter x1, waiting for transfers between devices: 0.01 us -> 31.3 us  [body(): lax.psum_scatter(acc_down.astype(jnp.bfloat16), 'dp', scatter_dimension=1...]
    all_gather x1, waiting for transfers between devices: 0.03 us -> 28.6 us  [body(): lax.all_gather(w_up, 'dp', axis=0, tiled=True)]
    all_gather x1, waiting for transfers between devices: 20.5 us -> 35.8 us  [body(): lax.all_gather(w_down, 'dp', axis=1, tiled=True)]
    unnamed x16 -> x17, waiting for transfers between devices: 109 us -> 107 us
  transfers between devices with their start and end apart: 14 -> 15, of which waited for: 8 -> 12; matrix products, arithmetic and copies ran while one was open for 19% -> 22% of each run, Pallas kernels for 0% -> 0%
where the time goes in v1:
time: 952 us; the launch traced here: 940 us
  waiting for transfers between devices  484 us (51%)
  blocking collectives  174 us (18%)
  local copies, waits for them, and re-layouts  122 us (13%)
  matrix products  91.6 us (10%)
  other arithmetic  51.8 us (5%)
  between operations  15.6 us (2%)
    unnamed x17, waiting for transfers between devices  107 us
    psum x1, blocking collectives, body(): head_sums = lax.psum((table_acc, qv_acc, up_bias_acc), 'dp')  57.7 us
    reduce_scatter x1, waiting for transfers between devices, body(): lax.psum_scatter(acc_query.astype(jnp.bfloat16), 'dp', scatter_dimension=...  57 us
    reduce_scatter x1, waiting for transfers between devices, body(): lax.psum_scatter(acc_key.astype(jnp.bfloat16), 'dp', scatter_dimension=0,...  56.9 us
    psum x1, waiting for transfers between devices, body(): grad_normed_one = lax.psum(token_terms, 'mp')  53 us
    reduce_scatter x1, waiting for transfers between devices, body(): lax.psum_scatter(acc_value.astype(jnp.bfloat16), 'dp', scatter_dimension=...  38.8 us
    psum x1, waiting for transfers between devices, body(): grad_normed_two = lax.psum(lifted, 'mp')  38.5 us
    all_gather x1, waiting for transfers between devices, body(): lax.all_gather(w_down, 'dp', axis=1, tiled=True)  35.8 us
  transfers between devices with their start and end apart: 15, of which 12 were waited for; matrix products, arithmetic and copies ran while one was open for 22% of the time, Pallas kernels for 0%

profile of v1, /device:TPU:0, one launch (start us, length us, event | category | flops | bytes accessed | tf_op | source)
XLA Modules:
  0.0 940.4 jit_solution(11313384894183692606)
XLA Ops:
  7.2 23.3 %all-gather.2 = bf16[16,32,2]{1,2,0:T(2,128)(2,1)S(1)} all-gather(bf16[1,32,2]{1,2,0:T(2,128)(2,1)} %bitcast.271), channel_id=1, replica_groups=mesh['dp'=16,'mp'=2] {'dp'}, dimensions={0}, use_global_device_ids=true | all-gather | bytes 2176 | tf_op jit(solution)/shard_map/all_gather | solution.py:137
  30.6 17.7 %all-gather.3 = bf16[16,32,4]{1,2,0:T(4,128)(2,1)S(1)} all-gather(bf16[1,32,4]{1,2,0:T(4,128)(2,1)} %bitcast.270), channel_id=1, replica_groups=mesh['dp'=16,'mp'=2] {'dp'}, dimensions={0}, use_global_device_ids=true | all-gather | bytes 4352 | tf_op jit(solution)/shard_map/all_gather | solution.py:138
  55.0 19.4 %all_gather.27 = bf16[512,256]{1,0:T(8,128)(2,1)S(1)} all-gather(bf16[32,256]{1,0:T(8,128)(2,1)S(1)} %copy-done.58), channel_id=1, replica_groups=mesh['dp'=16,'mp'=2] {'dp'}, dimensions={0}, use_global_device_ids=true | all-gather | bytes 278528 | tf_op jit(solution)/shard_map/all_gather | solution.py:131
  74.4 18.2 %all_gather.28 = bf16[512,256]{1,0:T(8,128)(2,1)S(1)} all-gather(bf16[32,256]{1,0:T(8,128)(2,1)S(1)} %copy-done.59), channel_id=1, replica_groups=mesh['dp'=16,'mp'=2] {'dp'}, dimensions={0}, use_global_device_ids=true | all-gather | bytes 278528 | tf_op jit(solution)/shard_map/all_gather | solution.py:132
  92.6 19.4 %all_gather.26 = bf16[512,256]{1,0:T(8,128)(2,1)S(1)} all-gather(bf16[32,256]{1,0:T(8,128)(2,1)S(1)} %copy-done.60), channel_id=1, replica_groups=mesh['dp'=16,'mp'=2] {'dp'}, dimensions={0}, use_global_device_ids=true | all-gather | bytes 278528 | tf_op jit(solution)/shard_map/all_gather | solution.py:133
  123.5 3.2 copy.265
  128.8 18.4 %all_gather.29 = bf16[256,512]{0,1:T(8,128)(2,1)S(1)} all-gather(bf16[256,32]{0,1:T(8,128)(2,1)S(1)} %copy-done.61), channel_id=1, replica_groups=mesh['dp'=16,'mp'=2] {'dp'}, dimensions={1}, use_global_device_ids=true | all-gather | bytes 278528 | tf_op jit(solution)/shard_map/all_gather | solution.py:134
  181.9 3.2 copy.278
  216.1 3.6 all-gather.15.cloned.1.call-done
  228.0 3.2 add_add_fusion.5
  231.2 28.6 %all-gather.9.cloned.1.call-done = bf16[512,1024]{1,0:T(8,128)(2,1)} async-done(((bf16[32,1024]{1,0:T(8,128)(2,1)}), bf16[512,1024]{1,0:T(8,128)(2,1)}) %all-gather.9.cloned.1.call-update) | async-done | bytes 1048592 | tf_op jit(solution)/shard_map/all_gather | solution.py:135
  259.8 3.1 fusion.87
  262.9 35.8 %all-gather.11.cloned.1.call-done = bf16[1024,512]{0,1:T(8,128)(2,1)} async-done(((bf16[1024,32]{0,1:T(8,128)(2,1)}), bf16[1024,512]{0,1:T(8,128)(2,1)}) %all-gather.11.cloned.1.call-update) | async-done | bytes 1048592 | tf_op jit(solution)/shard_map/all_gather | solution.py:136
  298.7 3.5 convert_reduce_fusion
  304.5 9.1 fusion.4
  317.7 3.0 convolution_convert_fusion.5
  330.6 38.5 %all-reduce.11.cloned.1.call-done = (f32[392,512]{1,0:T(8,128)}, f32[392,512]{1,0:T(8,128)}) async-done(((f32[392,512]{1,0:T(8,128)}, f32[392,512]{1,0:T(8,128)}), (f32[392,512]{1,0:T(8,128)}, f32[392,512]{1,0:T(8,128)})) %all-reduce.11.cloned.1.call-update) | async-done | bytes 1605648 | tf_op jit(solution)/shard_map/psum | solution.py:204
  369.1 3.1 multiply_reduce_fusion.8
  372.1 33.9 %all-reduce.13.cloned.1.call-done = (bf16[392,512]{1,0:T(8,128)(2,1)}, bf16[392,512]{1,0:T(8,128)(2,1)}) async-done(((bf16[392,512]{1,0:T(8,128)(2,1)}, bf16[392,512]{1,0:T(8,128)(2,1)}), (bf16[392,512]{1,0:T(8,128)(2,1)}, bf16[392,512]{1,0:T(8,128)(2,1)})) %all-reduce.13.cloned.1.call-update) | async-done | bytes 802832 | tf_op jit(solution)/shard_map/psum | solution.py:180
  406.0 4.3 fusion.90
  425.7 2.8 copy.284
  436.6 2.8 copy.300
  439.5 3.1 convert_reduce_fusion.2
  496.2 31.3 %reduce-scatter.23.cloned.1.call-done = bf16[1024,32]{0,1:T(8,128)(2,1)} async-done(((bf16[1024,512]{0,1:T(8,128)(2,1)}), bf16[1024,32]{0,1:T(8,128)(2,1)}) %reduce-scatter.23.cloned.1.call-update) | async-done | bytes 65552 | tf_op jit(solution)/shard_map/reduce_scatter | solution.py:302
  546.2 57.7 %all-reduce.1 = (f32[2,256]{1,0:T(2,128)}, f32[1024]{0:T(1024)}, f32[8,169]{1,0:T(8,128)}) all-reduce(f32[2,256]{1,0:T(2,128)S(1)} %maximum_add_fusion, f32[1024]{0:T(1024)S(1)} %add.525, f32[8,169]{1,0:T(8,128)S(1)} %fusion.56), channel_id=1, replica_groups=mesh['dp'=16,'mp'=2] {'dp'}, use_global_device_ids=true, to_apply=%region_54.55 | all-reduce | flops 2888 | bytes 23104 | tf_op jit(solution)/shard_map/psum | solution.py:312
  605.3 38.8 %reduce-scatter.17.cloned.1.call-done = bf16[32,256]{1,0:T(8,128)(2,1)} async-done(((bf16[512,256]{1,0:T(8,128)(2,1)}), bf16[32,256]{1,0:T(8,128)(2,1)}) %reduce-scatter.17.cloned.1.call-update) | async-done | bytes 16400 | tf_op jit(solution)/shard_map/reduce_scatter | solution.py:293
  645.4 57.0 %reduce-scatter.13.cloned.1.call-done = bf16[32,256]{1,0:T(8,128)(2,1)} async-done(((bf16[512,256]{1,0:T(8,128)(2,1)}), bf16[32,256]{1,0:T(8,128)(2,1)}) %reduce-scatter.13.cloned.1.call-update) | async-done | bytes 16400 | tf_op jit(solution)/shard_map/reduce_scatter | solution.py:287
  703.8 56.9 %reduce-scatter.15.cloned.1.call-done = bf16[32,256]{1,0:T(8,128)(2,1)} async-done(((bf16[512,256]{1,0:T(8,128)(2,1)}), bf16[32,256]{1,0:T(8,128)(2,1)}) %reduce-scatter.15.cloned.1.call-update) | async-done | bytes 16400 | tf_op jit(solution)/shard_map/reduce_scatter | solution.py:290
  762.0 53.0 %all-reduce.9.cloned.1.call-done = (f32[392,512]{1,0:T(8,128)}, f32[392,512]{1,0:T(8,128)}) async-done(((f32[392,512]{1,0:T(8,128)}, f32[392,512]{1,0:T(8,128)}), (f32[392,512]{1,0:T(8,128)}, f32[392,512]{1,0:T(8,128)})) %all-reduce.9.cloned.1.call-update) | async-done | bytes 1605648 | tf_op jit(solution)/shard_map/psum | solution.py:278
  818.4 2.7 add_convert_fusion.5
  825.5 48.5 %reduce-scatter.25.cloned.1.call-done = bf16[32,2]{1,0:T(8,128)(2,1)} async-done(((bf16[512,2]{1,0:T(8,128)(2,1)}), bf16[32,2]{1,0:T(8,128)(2,1)}) %reduce-scatter.25.cloned.1.call-update) | async-done | bytes 144
  875.4 56.6 %reduce-scatter.27.cloned.1.call-done = bf16[32,4]{1,0:T(8,128)(2,1)} async-done(((bf16[512,4]{1,0:T(8,128)(2,1)}), bf16[32,4]{1,0:T(8,128)(2,1)}) %reduce-scatter.27.cloned.1.call-update) | async-done | bytes 272
  (433 shorter events, 220.9 us)
Async XLA Ops:
  7.2 46.4 %copy-start = (bf16[8,169]{1,0:T(8,128)(2,1)S(1)}, bf16[8,169]{1,0:T(8,128)(2,1)}, u32[]{:S(2)}) copy-start(bf16[8,169]{1,0:T(8,128)(2,1)} %param.51) | copy-start | bytes 8116
  7.2 202.9 %all-gather.13.cloned.1.call-start = ((), (), s32[]{:S(2)}) async-start(), calls=%async_computation.16 | async-start | bytes 2408448 | tf_op jit(solution)/shard_map/all_gather | solution.py:173
  52.7 21.7 %copy-start.59 = (bf16[32,256]{1,0:T(8,128)(2,1)S(1)}, bf16[32,256]{1,0:T(8,128)(2,1)}, u32[]{:S(2)}) copy-start(bf16[32,256]{1,0:T(8,128)(2,1)} %param.42) | copy-start | bytes 49156
  52.7 39.9 %copy-start.60 = (bf16[32,256]{1,0:T(8,128)(2,1)S(1)}, bf16[32,256]{1,0:T(8,128)(2,1)}, u32[]{:S(2)}) copy-start(bf16[32,256]{1,0:T(8,128)(2,1)} %param.43) | copy-start | bytes 49156
  53.5 39.1 %copy-start.62 = (s32[2401]{0:T(1024)}, s32[2401]{0:T(1024)S(1)}, u32[]{:S(2)}) copy-start(s32[2401]{0:T(1024)S(1)} %eq.35) | copy-start | bytes 28816
  74.4 42.7 %copy-start.11 = (bf16[512,256]{1,0:T(8,128)(2,1)}, bf16[512,256]{1,0:T(8,128)(2,1)S(1)}, u32[]{:S(2)}) copy-start(bf16[512,256]{1,0:T(8,128)(2,1)S(1)} %all_gather.27) | copy-start | bytes 786436
  92.6 20.6 %copy-start.15 = (bf16[512,256]{1,0:T(8,128)(2,1)}, bf16[512,256]{1,0:T(8,128)(2,1)S(1)}, u32[]{:S(2)}) copy-start(bf16[512,256]{1,0:T(8,128)(2,1)S(1)} %all_gather.28) | copy-start | bytes 786436
  123.5 5.3 copy-start.61
  147.2 4.8 copy-start.9
  152.0 67.7 %all-gather.15.cloned.1.call-start = ((), (), s32[]{:S(2)}) async-start(), calls=%async_computation.17 | async-start | bytes 2408448 | tf_op jit(solution)/shard_map/all_gather | solution.py:173
  193.7 66.1 %all-gather.9.cloned.1.call-start = ((), (), s32[]{:S(2)}) async-start(), calls=%async_computation.8 | async-start | bytes 1114112 | tf_op jit(solution)/shard_map/all_gather | solution.py:135
  194.4 104.3 %all-gather.11.cloned.1.call-start = ((), (), s32[]{:S(2)}) async-start(), calls=%async_computation.9 | async-start | bytes 1114112 | tf_op jit(solution)/shard_map/all_gather | solution.py:136
  195.0 174.0 %all-reduce.11.cloned.1.call-start = ((), (), s32[]{:S(2)}) async-start(), calls=%async_computation.21 | async-start | bytes 3211264 | tf_op jit(solution)/shard_map/psum | solution.py:204
  259.8 38.9 %copy-start.71 = (f32[1024]{0:T(1024)S(1)}, f32[1024]{0:T(1024)}, u32[]{:S(2)}) copy-start(f32[1024]{0:T(1024)} %convert_element_type.258) | copy-start | bytes 12292
  304.5 9.1 copy-start.27
  304.5 9.1 copy-start.74
  317.7 88.4 %all-reduce.13.cloned.1.call-start = ((), (), s32[]{:S(2)}) async-start(), calls=%async_computation.22 | async-start | bytes 1605632 | tf_op jit(solution)/shard_map/psum | solution.py:180
  322.1 172.6 %reduce-scatter.21.cloned.1.call-start = ((), (), s32[]{:S(2)}) async-start(), calls=%async_computation.14 | async-start | bytes 1114112 | tf_op jit(solution)/shard_map/reduce_scatter | solution.py:299
  326.5 201.0 %reduce-scatter.23.cloned.1.call-start = ((), (), s32[]{:S(2)}) async-start(), calls=%async_computation.15 | async-start | bytes 1114112 | tf_op jit(solution)/shard_map/reduce_scatter | solution.py:302
  330.5 273.4 %reduce-scatter.19.cloned.1.call-start = ((), (), s32[]{:S(2)}) async-start(), calls=%async_computation.13 | async-start | bytes 278528 | tf_op jit(solution)/shard_map/reduce_scatter | solution.py:296
  406.0 5.2 copy-start.10
  410.3 6.5 copy-start.6
  454.1 6.6 copy-start.34
  466.6 177.5 %reduce-scatter.17.cloned.1.call-start = ((), (), s32[]{:S(2)}) async-start(), calls=%async_computation.12 | async-start | bytes 278528 | tf_op jit(solution)/shard_map/reduce_scatter | solution.py:293
  471.0 4.6 copy-start.14
  471.0 231.4 %reduce-scatter.13.cloned.1.call-start = ((), (), s32[]{:S(2)}) async-start(), calls=%async_computation.10 | async-start | bytes 278528 | tf_op jit(solution)/shard_map/reduce_scatter | solution.py:287
  478.2 282.5 %reduce-scatter.15.cloned.1.call-start = ((), (), s32[]{:S(2)}) async-start(), calls=%async_computation.11 | async-start | bytes 278528 | tf_op jit(solution)/shard_map/reduce_scatter | solution.py:290
  479.8 335.2 %all-reduce.9.cloned.1.call-start = ((), (), s32[]{:S(2)}) async-start(), calls=%async_computation.20 | async-start | bytes 3211264 | tf_op jit(solution)/shard_map/psum | solution.py:278
  490.6 383.4 %reduce-scatter.25.cloned.1.call-start = ((), (), s32[]{:S(2)}) async-start(), calls=%async_computation.18 | async-start | bytes 139264
  534.0 5.8 copy-start.55
  818.3 113.7 %reduce-scatter.27.cloned.1.call-start = ((), (), s32[]{:S(2)}) async-start(), calls=%async_computation.19 | async-start | bytes 139264
  824.2 109.3 %copy-start.1 = (bf16[8,169]{1,0:T(8,128)(2,1)S(1)}, bf16[8,169]{1,0:T(8,128)(2,1)}, u32[]{:S(2)}) copy-start(bf16[8,169]{1,0:T(8,128)(2,1)} %param.51) | copy-start | bytes 8116
  (60 other events, 135.8 us)
Sparse Core Ops, SparseCore 0:
  152.1 25.8 all-gather.12
  193.8 25.8 all-gather.14
  221.9 37.8 all-gather.8
  261.9 36.8 all-gather.10
  317.8 51.2 all-reduce.10
  371.3 34.7 all-reduce.12
  409.7 57.5 reduce-scatter.20
  470.9 56.6 reduce-scatter.22
  531.1 54.8 reduce-scatter.18
  589.3 54.7 reduce-scatter.16
  647.6 54.7 reduce-scatter.12
  705.8 54.7 reduce-scatter.14
  763.6 51.3 all-reduce.8
  818.4 55.5 reduce-scatter.24
  877.4 54.6 reduce-scatter.26
